TPU v7x, 512 devices: a whole 4x4x16 slice. The times are simulated.
512 devices in a mesh: island: 8 (over x, core), dp: 2 (over y_lo), expert: 32 (over y_hi, z).
Axes of the slice: x: 4, y: 4 (y_hi: 2, y_lo: 2; y = y_hi * 2 + y_lo), z: 16, core: 2. Of those that a mesh axis runs over, the one named last changes fastest.
Arguments:
- theta: bfloat16 [8, 32, 384, 2048], P('island', 'expert', 'dp'), may hold values from -7.5 to 7.5
- first_moment: bfloat16 [8, 32, 384, 2048], P('island', 'expert', 'dp'), may hold values from -0.119628906 to 0.119628906
- second_moment: bfloat16 [8, 32, 384, 2048], P('island', 'expert', 'dp'), may hold values from 9.9658966e-05 to 0.0099487305
- anchor: float32 [32, 384, 2048], P('expert', 'dp', 'island'), may hold values from -4.5 to 4.5
- momentum: float32 [32, 384, 2048], P('expert', 'dp', 'island'), may hold values from -1.8 to 1.8
- cotangent: bfloat16 [65536, 2048], P(('island', 'dp', 'expert')), may hold values from -6 to 6
- weights: float32 [65536, 8], P(('island', 'dp', 'expert')), may hold values from 0.05 to 0.3
- expert_ids: int32 [65536, 8], P(('island', 'dp', 'expert')), may hold values from 0 to 127, as said below
- expert_counts: int32 [512, 16], P(('island', 'dp', 'expert')), may hold values from 1 to 16, as said below
- hidden_saved: bfloat16 [8, 2, 32, 512, 384], P('island', 'dp', 'expert'), may hold values from -6 to 6
Outputs:
- anchor_new: float32 [32, 384, 2048], P('expert', 'dp', 'island')
- momentum_new: float32 [32, 384, 2048], P('expert', 'dp', 'island')
- d_hidden: bfloat16 [8, 2, 32, 512, 384], P('island', 'dp', 'expert')
Inputs may be any that keep to these rules, and one draw needn't show every extreme that they name: `expert_ids`: in each block of 128 rows a row's ids are distinct, every id below 16 is named by 1 to 16 pairs of the block, and those counts equal expert_counts of the block. expert_counts[b, e] is the number of pairs of block b naming expert e.
All inputs are finite; a program needn't handle non-finite values.
Results may differ from a plain program's by a relative error of at most 0.014.
Values may be sent and summed in bfloat16 or wider, within the bound.
A program may use at most 64 MiB of HBM per device.

v0:
```python
import jax
import jax.numpy as jnp
from jax import lax
from jax.sharding import PartitionSpec as P

FF = 768
CAP = 16


beta_one = 0.9
beta_two = 0.95
adam_epsilon = 1e-08
inner_rate = 0.1
decay_rate = 0.1
outer_beta = 0.9
outer_rate = 0.7


def pack_rows(capacity, cotangent, weights, expert_ids, counts):
    window_experts = counts.shape[0]
    route_width = expert_ids.shape[1]
    flat_ids = expert_ids.reshape(-1)
    match_table = (
        flat_ids[:, None] == jnp.arange(window_experts, dtype=jnp.int32)[None, :]
    ).astype(jnp.int32)
    earlier = jnp.cumsum(match_table, axis=0) - match_table
    pair_rank = jnp.sum(earlier * match_table, axis=1)
    slot_limit = jnp.sum(match_table * counts[None, :], axis=1)
    is_live = pair_rank < slot_limit
    slot_index = jnp.where(is_live, flat_ids * capacity + pair_rank, window_experts * capacity)
    source_row = jnp.arange(flat_ids.shape[0], dtype=jnp.int32) // route_width
    slot_source = (
        jnp.zeros((window_experts * capacity + 1,), jnp.int32).at[slot_index].set(source_row)[:-1]
    )
    live_weight = jnp.where(is_live, weights.reshape(-1), jnp.zeros_like(weights.reshape(-1)))
    slot_scale = (
        jnp.zeros((window_experts * capacity + 1,), jnp.float32)
        .at[slot_index]
        .set(live_weight)[:-1]
    )
    packed = (cotangent[slot_source].astype(jnp.float32) * slot_scale[:, None]).astype(jnp.bfloat16)
    return packed.reshape(window_experts, capacity, cotangent.shape[1])


def per_device(
    theta,
    first_moment,
    second_moment,
    anchor,
    momentum,
    cotangent,
    weights,
    expert_ids,
    expert_counts,
    hidden_saved,
):
    capacity = CAP
    scale = FF ** (-0.5)
    packed = pack_rows(capacity, cotangent, weights, expert_ids, expert_counts[0])
    width_d = packed.shape[2]
    doubled = jnp.repeat(packed, 2, axis=0)
    received = lax.all_to_all(doubled, "expert", split_axis=0, concat_axis=0, tiled=True)
    slot_rows = received.reshape(-1, width_d)
    saved = hidden_saved.reshape(slot_rows.shape[0], hidden_saved.shape[-1])
    local_theta = theta.reshape(theta.shape[2], width_d)
    d_hidden = (
        scale
        * lax.dot_general(
            slot_rows,
            lax.all_gather(local_theta, "dp", axis=0, tiled=True),
            (((1,), (1,)), ((), ())),
            preferred_element_type=jnp.float32,
        )
    ).astype(jnp.bfloat16)
    grad = lax.psum_scatter(
        (
            scale
            * lax.dot_general(
                saved, slot_rows, (((0,), (0,)), ((), ())), preferred_element_type=jnp.float32
            )
        ).astype(jnp.bfloat16),
        "dp",
        scatter_dimension=0,
        tiled=True,
    ).astype(jnp.float32)
    first_new = (
        beta_one * first_moment.reshape(grad.shape).astype(jnp.float32) + (1.0 - beta_one) * grad
    )
    second_new = (
        beta_two * second_moment.reshape(grad.shape).astype(jnp.float32)
        + (1.0 - beta_two) * grad * grad
    )
    theta_wide = local_theta.astype(jnp.float32)
    step_size = first_new / (jnp.sqrt(second_new) + adam_epsilon) + decay_rate * theta_wide
    theta_new = (theta_wide - inner_rate * step_size).astype(jnp.bfloat16)
    local_anchor = anchor.reshape(anchor.shape[1], anchor.shape[2])
    island_count = lax.axis_size("island")
    full_anchor = lax.all_gather(local_anchor, "island", axis=1, tiled=True)
    island_delta = full_anchor - theta_new.astype(jnp.float32)
    summed_delta = lax.psum_scatter(island_delta, "island", scatter_dimension=1, tiled=True)
    mean_delta = summed_delta / island_count
    momentum_new = outer_beta * momentum.reshape(mean_delta.shape) + mean_delta
    anchor_new = local_anchor - outer_rate * (mean_delta + outer_beta * momentum_new)
    return (
        anchor_new.reshape(anchor.shape),
        momentum_new.reshape(momentum.shape),
        d_hidden.reshape(hidden_saved.shape),
    )


def solution(mesh):
    return jax.shard_map(
        per_device,
        mesh=mesh,
        in_specs=(
            P("island", "expert", "dp", None),
            P("island", "expert", "dp", None),
            P("island", "expert", "dp", None),
            P("expert", "dp", "island"),
            P("expert", "dp", "island"),
            P(("island", "dp", "expert"), None),
            P(("island", "dp", "expert"), None),
            P(("island", "dp", "expert"), None),
            P(("island", "dp", "expert"), None),
            P("island", "dp", "expert", None, None),
        ),
        out_specs=(
            P("expert", "dp", "island"),
            P("expert", "dp", "island"),
            P("island", "dp", "expert", None, None),
        ),
        check_vma=False,
    )
```

profile of v0, /device:TPU:1, one launch (start us, length us, event | category | flops | bytes accessed | tf_op | source)
XLA Modules:
  0.0 271.0 jit_solution(6349734036679307059)
XLA Ops:
  8.0 0.0 copy-start
  8.0 0.0 reduce-scatter.7.cloned.1.call-start
  8.1 0.7 broadcast_multiply_fusion
  8.8 0.8 copy.41
  9.6 0.1 eq.29
  9.7 0.1 eq.25
  9.8 0.1 copy.45
  9.9 0.1 mul.113
  10.0 4.5 %reduce-window.6 = s32[16,8,128]{2,1,0:T(8,128)S(1)} reduce-window(s32[16,8,128]{2,1,0:T(8,128)S(1)} %fusion.27, s32[]{:T(128)} %constant.19.clone.1), window={size=1x1x128 pad=0_0x0_0x127_0}, to_apply=%region_0.0 | reduce-window | flops 2080768 | bytes 131076 | tf_op jit(solution)/shard_map/reduce-window
  14.5 0.1 slice.18
  14.6 0.1 copy.43
  14.8 0.1 copy.44
  14.8 0.1 broadcast_add_fusion
  14.9 0.7 select_reduce_fusion
  15.7 4.3 %scatter_custom_fusion = s32[257]{0:T(512)S(1)} fusion(s32[1024]{0:T(1024)S(1)} %bitcast.86, s32[1024]{0:T(1024)S(1)} %add_select_fusion, s32[]{:T(128)} %constant.19.clone.1), kind=kCustom, calls=%fused_computation.54 | custom fusion | bytes 1032 | tf_op jit(solution)/shard_map/scatter | solution.py:33
  20.0 0.8 copy.46
  20.8 0.1 reshape.113
  20.9 4.3 %scatter_custom_fusion.1 = f32[257]{0:T(512)S(1)} fusion(s32[1024]{0:T(1024)S(1)} %bitcast.87, f32[1024]{0:T(1024)S(1)} %compare_select_fusion.2, f32[]{:T(128)} %constant.49.clone.1), kind=kCustom, calls=%fused_computation.52 | custom fusion | bytes 1032 | tf_op jit(solution)/shard_map/scatter | solution.py:39
  25.2 0.1 mul.114
  25.3 1.4 gather_fusion
  26.7 0.2 fusion.8
  26.9 0.3 broadcast_in_dim.28
  27.2 114.8 %all_to_all.5 = bf16[32,16,2048]{2,1,0:T(8,128)(2,1)S(1)} all-to-all(bf16[32,16,2048]{2,1,0:T(8,128)(2,1)S(1)} %bitcast.78), channel_id=1, replica_groups=mesh['island'=8,'dp'=2,'expert'=32] {'expert'}, dimensions={0} | all-to-all | bytes 4194304 | tf_op jit(solution)/shard_map/all_to_all | solution.py:62
  142.0 1.3 copy-done.3
  143.3 1.3 fusion
  144.6 0.0 copy-start.5
  144.6 1.7 copy.51
  146.3 0.0 reduce-scatter.7.cloned.1.call-update
  146.3 0.0 all-gather.5.cloned.1.call-start
  146.4 0.9 copy.37
  147.2 0.0 all-gather.5.cloned.1.call-update
  147.3 0.0 all-gather.7.cloned.1.call-start
  147.3 0.5 all-gather.7.cloned.1.call-update
  147.9 0.0 reduce-scatter.5.cloned.1.call-start
  147.9 0.5 copy.39
  148.4 1.4 copy.40
  149.9 2.3 copy.47
  152.2 26.5 %reduce-scatter.7.cloned.1.call-done = bf16[192,2048]{1,0:T(8,128)(2,1)} async-done(((bf16[384,2048]{1,0:T(8,128)(2,1)}), bf16[192,2048]{1,0:T(8,128)(2,1)}) %reduce-scatter.7.cloned.1.call-update) | async-done | bytes 786448
  178.7 2.2 copy.52
  180.9 5.3 %bitcast_subtract_fusion = f32[192,2048]{0,1:T(8,128)} fusion(f32[1,192,2048]{1,2,0:T(8,128)} %all-gather.5.cloned.1.call-done, bf16[1,1,192,2048]{2,3,1,0:T(8,128)(2,1)} %copy.47, bf16[192,2048]{0,1:T(8,128)(2,1)} %copy.52, bf16[1,1,192,2048]{2,3,1,0:T(8,128)(2,1)S(1)} %copy.40, bf16[1,1,192,2048]{2,3,1,0:T(8,128)(2,1)S(1)} %copy.39), kind=kLoop, calls=%fused_computation.18 | loop fusion | flops 7864320 | bytes 6291456 | tf_op jit(solution)/shard_map/sub | solution.py:99
  186.1 0.0 reduce-scatter.5.cloned.1.call-update
  186.2 1.2 copy.48
  187.4 29.9 %all-gather.7.cloned.1.call-done = bf16[1,1,384,2048]{3,2,1,0:T(8,128)(2,1)} async-done(((bf16[1,1,192,2048]{3,2,1,0:T(8,128)(2,1)}), bf16[1,1,384,2048]{3,2,1,0:T(8,128)(2,1)}) %all-gather.7.cloned.1.call-update) | async-done | bytes 1572880 | tf_op jit(solution)/shard_map/all_gather | solution.py:70
  217.3 3.4 %fusion.18 = bf16[1,1,1,512,384]{4,3,2,1,0:T(8,128)(2,1)} fusion(bf16[512,2048]{1,0:T(8,128)(2,1)S(1)} %bitcast.81, bf16[1,1,384,2048]{3,2,1,0:T(8,128)(2,1)} %all-gather.7.cloned.1.call-done), kind=kOutput, calls=%fused_computation.24 | convolution fusion | flops 805699584 | bytes 4063232 | tf_op jit(solution)/shard_map/dot_general | solution.py:68
  220.7 40.1 %reduce-scatter.5.cloned.1.call-done = f32[192,256]{0,1:T(8,128)} async-done(((f32[192,2048]{0,1:T(8,128)}), f32[192,256]{0,1:T(8,128)}) %reduce-scatter.5.cloned.1.call-update) | async-done | bytes 196624 | tf_op jit(solution)/shard_map/reduce_scatter | solution.py:100
  260.8 1.0 fusion.23
  261.9 0.8 copy.50
  262.6 0.8 copy.49
  (21 shorter events, 0.1 us)
Async XLA Ops:
  8.0 17.3 %copy-start = (bf16[128,2048]{1,0:T(8,128)(2,1)S(1)}, bf16[128,2048]{1,0:T(8,128)(2,1)}, u32[]{:S(2)}) copy-start(bf16[128,2048]{1,0:T(8,128)(2,1)} %param.15) | copy-start | bytes 1572868
  8.0 170.7 %reduce-scatter.7.cloned.1.call-start = ((), (), s32[]{:S(2)}) async-start(), calls=%async_computation.6 | async-start | bytes 2359296
  27.2 116.1 %copy-start.6 = (bf16[1,1,1,512,384]{4,3,2,1,0:T(8,128)(2,1)S(1)}, bf16[1,1,1,512,384]{4,3,2,1,0:T(8,128)(2,1)}, u32[]{:S(2)}) copy-start(bf16[1,1,1,512,384]{4,3,2,1,0:T(8,128)(2,1)} %param.19) | copy-start | bytes 1179652
  142.0 1.4 copy-start.3
  144.6 1.7 copy-start.5
  146.3 1.6 copy-start.1
  146.3 34.6 %all-gather.5.cloned.1.call-start = ((), (), s32[]{:S(2)}) async-start(), calls=%async_computation.4 | async-start | bytes 2359296 | tf_op jit(solution)/shard_map/all_gather | solution.py:98
  147.3 70.0 %all-gather.7.cloned.1.call-start = ((), (), s32[]{:S(2)}) async-start(), calls=%async_computation.5 | async-start | bytes 2359296 | tf_op jit(solution)/shard_map/all_gather | solution.py:70
  147.9 113.0 %reduce-scatter.5.cloned.1.call-start = ((), (), s32[]{:S(2)}) async-start(), calls=%async_computation.3 | async-start | bytes 2359296 | tf_op jit(solution)/shard_map/reduce_scatter | solution.py:100
  186.1 31.2 %copy-start.4 = (bf16[32,16,2048]{2,1,0:T(8,128)(2,1)S(1)}, bf16[32,16,2048]{2,1,0:T(8,128)(2,1)}, u32[]{:S(2)}) copy-start(bf16[32,16,2048]{2,1,0:T(8,128)(2,1)} %copy-done.3) | copy-start | bytes 6291460
  187.4 73.5 %copy-start.2 = (f32[1,192,256]{1,2,0:T(8,128)S(1)}, f32[1,192,256]{1,2,0:T(8,128)}, u32[]{:S(2)}) copy-start(f32[1,192,256]{1,2,0:T(8,128)} %copy.37) | copy-start | bytes 589828
Sparse Core Ops, SparseCore 0:
  146.4 32.1 reduce-scatter.6
Sparse Core Ops, SparseCore 1:
  148.9 29.3 all-gather.4
  180.2 37.0 all-gather.6
  220.3 40.5 reduce-scatter.4
where the time goes:
time: 272 us; the launch traced here: 271 us
  blocking collectives  115 us (42%)
  waiting for transfers between devices  97.1 us (36%)
  local copies, waits for them, and re-layouts  25.8 us (9%)
  between operations  15.8 us (6%)
  other arithmetic  12.7 us (5%)
  matrix products  4.73 us (2%)
    all_to_all x1, blocking collectives, per_device(): lax.all_to_all(doubled, 'expert', split_axis=0, concat_axis=0, tiled=True)  115 us
    reduce_scatter x1, waiting for transfers between devices, per_device(): lax.psum_scatter(island_delta, 'island', scatter_dimension=1, tiled=True)  40.1 us
    all_gather x1, waiting for transfers between devices, per_device(): lax.all_gather(local_theta, 'dp', axis=0, tiled=True)  29.9 us
    unnamed x5, waiting for transfers between devices  27.1 us
    unnamed x25, local copies, waits for them, and re-layouts  14.7 us
  transfers between devices with their start and end apart: 4, of which 3 were waited for; matrix products, arithmetic and copies ran while one was open for 6% of the time, Pallas kernels for 0%

commit v1 on v0

v1 whole, which is shorter than its diff:
```python
import functools

import jax
import jax.numpy as jnp
from jax import lax
from jax.experimental import pallas as pl
from jax.experimental.pallas import tpu as pltpu
from jax.sharding import PartitionSpec as P

FF = 768
CAP = 16
HALVES = 2
GROUPS = 2
AHEAD = 2

beta_one = 0.9
beta_two = 0.95
adam_epsilon = 1e-08
inner_rate = 0.1
decay_rate = 0.1
outer_beta = 0.9
outer_rate = 0.7

MESH = pl.DeviceIdType.MESH
F32 = jnp.float32
BF16 = jnp.bfloat16


def dot(a, b, dims):
    return lax.dot_general(a, b, (dims, ((), ())), preferred_element_type=F32)


def body(
    n_island,
    n_expert,
    ids_ref,
    weights_ref,
    counts_ref,
    theta_hbm,
    first_hbm,
    second_hbm,
    anchor_hbm,
    momentum_hbm,
    cot_hbm,
    saved_hbm,
    anchor_out,
    momentum_out,
    hidden_out,
    cot,
    saved,
    saved_t,
    first,
    second,
    anchor,
    momentum,
    picks,
    packed,
    slots,
    thetas,
    partial,
    partner_partial,
    new_theta,
    all_theta,
    hidden_acc,
    load_sem,
    saved_sem,
    theta_sem,
    send_sem,
    recv_sem,
    pass_send,
    pass_recv,
    theta_send,
    theta_recv,
    grad_send,
    grad_recv,
    island_send,
    island_recv,
):
    ring = n_expert // GROUPS
    pairs = ring // HALVES
    half_pairs = pairs // 2
    per_half = ring // HALVES
    experts = GROUPS * pairs
    rows = GROUPS * per_half * CAP
    width = cot.shape[1] // n_island
    theta_rows = thetas.shape[2]
    tokens = cot.shape[0]
    scale = FF ** (-0.5)

    island = lax.axis_index("island")
    dp = lax.axis_index("dp")
    me = lax.axis_index("expert")
    group = me // ring
    z = me % ring
    pair = z // HALVES
    half = z % HALVES
    partner = group * ring + pair * HALVES + (1 - half)
    other_dp = 1 - dp

    def columns(step):
        chunk = (island + 1 + step) % n_island
        return pl.ds(pl.multiple_of(chunk * width, width), width)

    loads = [
        pltpu.make_async_copy(src, dst, load_sem.at[k])
        for k, (src, dst) in enumerate(
            [
                (cot_hbm, cot),
                (first_hbm, first),
                (second_hbm, second),
                (anchor_hbm, anchor),
                (momentum_hbm, momentum),
            ]
        )
    ]
    loads[0].start()

    barrier = pltpu.get_barrier_semaphore()
    greeted = 0
    for other in range(GROUPS):
        for k in range(per_half):
            if other == 0 and k == 0:
                continue
            source_group = (group + other) % GROUPS
            source_z = (z + (2 * half - 1) * k + ring) % ring
            pl.semaphore_signal(
                barrier,
                inc=1,
                device_id={"expert": source_group * ring + source_z},
                device_id_type=MESH,
            )
            greeted += 1
    pl.semaphore_signal(barrier, inc=1, device_id={"expert": partner}, device_id_type=MESH)
    pl.semaphore_signal(barrier, inc=1, device_id={"dp": other_dp}, device_id_type=MESH)
    greeted += 2
    for k in range(1, n_island):
        pl.semaphore_signal(
            barrier, inc=1, device_id={"island": (island + k) % n_island}, device_id_type=MESH
        )
        greeted += 1

    def theta_load(step):
        return pltpu.make_async_copy(
            theta_hbm.at[:, columns(step)], thetas.at[step, dp], theta_sem.at[step]
        )

    for step in range(n_island):
        theta_load(step).start()

    def canonical(k):
        which = k // (GROUPS * per_half)
        other = (k // per_half) % GROUPS
        q = k % per_half
        source_z = (pair * HALVES - (per_half - 1) + per_half * which + q + ring) % ring
        return other * ring + source_z

    blocks = HALVES * GROUPS * per_half

    def load_saved(k, carry):
        pltpu.make_async_copy(
            saved_hbm.at[pl.ds(pl.multiple_of(canonical(k) * CAP, CAP), CAP)],
            saved.at[pl.ds(pl.multiple_of(k * CAP, CAP), CAP)],
            saved_sem,
        ).start()
        return carry

    lax.fori_loop(0, blocks, load_saved, 0)
    for load in loads[1:]:
        load.start()

    ids = ids_ref[...]
    weights = weights_ref[...]
    expert_of = lax.broadcasted_iota(jnp.int32, (experts, tokens), 0)
    named = jnp.zeros((experts, tokens), F32)
    weight = jnp.zeros((experts, tokens), F32)
    for k in range(ids.shape[0]):
        hit = ids[k : k + 1, :] == expert_of
        named = jnp.where(hit, 1.0, named)
        weight = jnp.where(hit, weights[k : k + 1, :], weight)
    before = (
        lax.broadcasted_iota(jnp.int32, (tokens, tokens), 0)
        < lax.broadcasted_iota(jnp.int32, (tokens, tokens), 1)
    )
    rank = dot(
        named.astype(BF16), jnp.where(before, 1.0, 0.0).astype(BF16), ((1,), (0,))
    ).astype(jnp.int32)
    diagonal = lax.broadcasted_iota(jnp.int32, (experts, experts), 0) == lax.broadcasted_iota(
        jnp.int32, (experts, experts), 1
    )
    count = jnp.sum(
        jnp.where(diagonal, counts_ref[...].astype(F32), 0.0), axis=1, keepdims=True
    ).astype(jnp.int32)
    rank = jnp.where((named > 0.0) & (rank < count), rank, CAP)
    slot_of = lax.broadcasted_iota(jnp.int32, (experts, CAP, tokens), 1)
    table = jnp.where(rank[:, None, :] == slot_of, weight[:, None, :], 0.0)
    table = table.reshape(experts * CAP, tokens)
    high = table.astype(BF16)
    rest = table - high.astype(F32)
    middle = rest.astype(BF16)
    picks[0] = high
    picks[1] = middle
    picks[2] = (rest - middle.astype(F32)).astype(BF16)

    own_row = (group * per_half + (1 - half) * (per_half - 1)) * CAP
    own_expert = group * pairs + pair

    def pack(step):
        chunk = cot[:, columns(step)]
        rows_out = sum(dot(picks[k], chunk, ((1,), (0,))) for k in range(3))
        packed[step] = rows_out.astype(BF16).reshape(experts, CAP, width)
        slots[step, half, pl.ds(pl.multiple_of(own_row, CAP), CAP), :] = packed[step, own_expert]

    def sends(step):
        copies = []
        for d in (half_pairs, *range(half_pairs - 1, 0, -1), *range(half_pairs + 1, pairs), 0):
            for other in range(GROUPS):
                if other == 0 and d == 0:
                    continue
                to_group = (group + other) % GROUPS
                to_pair = (pair + d) % pairs
                if d == 0:
                    to_half = half
                elif d == half_pairs:
                    to_half = 1 - half
                else:
                    to_half = 0 if d < half_pairs else 1
                place = (half - 2 * d + per_half - 1 - per_half * to_half + 3 * ring) % ring
                row = (group * per_half + place) * CAP
                copies.append(
                    pltpu.make_async_remote_copy(
                        packed.at[step, to_group * pairs + to_pair],
                        slots.at[step, to_half, pl.ds(pl.multiple_of(row, CAP), CAP)],
                        send_sem.at[step],
                        recv_sem.at[step],
                        device_id={"expert": to_group * ring + to_pair * HALVES + to_half},
                        device_id_type=MESH,
                    )
                )
        return copies

    def send(step):
        for copy in sends(step):
            copy.start()

    def arrived(step, sem):
        some = slots.at[step, 0, pl.ds(0, rows - CAP)]
        return pltpu.make_async_copy(some, some, sem.at[step])

    def pass_on(step):
        return pltpu.make_async_remote_copy(
            slots.at[step, half],
            slots.at[step, half],
            pass_send.at[step],
            pass_recv.at[step],
            device_id={"expert": partner},
            device_id_type=MESH,
        )

    def share_theta(step):
        return pltpu.make_async_remote_copy(
            thetas.at[step, dp],
            thetas.at[step, dp],
            theta_send.at[step],
            theta_recv.at[step],
            device_id={"dp": other_dp},
            device_id_type=MESH,
        )

    def share_grad(step):
        return pltpu.make_async_remote_copy(
            partial.at[step, other_dp],
            partner_partial.at[step],
            grad_send.at[step],
            grad_recv.at[step],
            device_id={"dp": other_dp},
            device_id_type=MESH,
        )

    def share_island(step):
        owner = (island + 1 + step) % n_island
        return pltpu.make_async_remote_copy(
            new_theta.at[step],
            all_theta.at[island],
            island_send.at[step],
            island_recv.at[island],
            device_id={"island": owner},
            device_id_type=MESH,
        )

    def contract(step):
        chunk = slots[step].reshape(HALVES * rows, width)
        product = (scale * dot(saved_t[...], chunk, ((1,), (0,)))).astype(BF16)
        partial[step, 0] = product[:theta_rows]
        partial[step, 1] = product[theta_rows:]
        share_grad(step).start()
        share_theta(step).wait_recv()
        full = thetas[step].reshape(2 * theta_rows, width)
        hidden_acc[...] += dot(chunk, full, ((1,), (1,)))

    def update(step):
        share_grad(step).wait_recv()
        grad = partial[step, dp].astype(F32) + partner_partial[step].astype(F32)
        first_new = beta_one * first[:, columns(step)].astype(F32) + (1.0 - beta_one) * grad
        second_new = (
            beta_two * second[:, columns(step)].astype(F32) + (1.0 - beta_two) * grad * grad
        )
        wide = thetas[step, dp].astype(F32)
        step_size = first_new / (jnp.sqrt(second_new) + adam_epsilon) + decay_rate * wide
        return (wide - inner_rate * step_size).astype(BF16)

    loads[0].wait()
    for step in range(AHEAD):
        pack(step)

    pl.semaphore_wait(barrier, greeted)
    for step in range(AHEAD):
        send(step)

    for step in range(n_island):
        theta_load(step).wait()
        share_theta(step).start()

    pltpu.make_async_copy(saved, saved, saved_sem).wait()
    saved_t[...] = saved[...].T
    hidden_acc[...] = jnp.zeros_like(hidden_acc)
    for load in loads[1:]:
        load.wait()

    def run(t, carry):
        @pl.when(t + AHEAD < n_island)
        def _():
            pack(t + AHEAD)
            send(t + AHEAD)

        @pl.when(t < n_island)
        def _():
            arrived(t, recv_sem).wait()
            pass_on(t).start()

        @pl.when((t >= 1) & (t <= n_island))
        def _():
            pass_on(t - 1).wait_recv()
            contract(t - 1)

        @pl.when(t >= 2)
        def _():
            fresh = update(t - 2)

            @pl.when(t < n_island + 1)
            def _():
                new_theta[t - 2] = fresh
                share_island(t - 2).start()

            @pl.when(t == n_island + 1)
            def _():
                all_theta[island] = fresh

        return carry

    lax.fori_loop(0, n_island + 2, run, 0)

    for k in range(blocks):
        at = pl.ds(pl.multiple_of(canonical(k) * CAP, CAP), CAP)
        hidden_out[at, :] = (scale * hidden_acc[k * CAP : (k + 1) * CAP, :]).astype(BF16)

    for k in range(1, n_island):
        source = (island + k) % n_island
        pltpu.make_async_copy(
            all_theta.at[source], all_theta.at[source], island_recv.at[source]
        ).wait()
    total = all_theta[0].astype(F32)
    for k in range(1, n_island):
        total += all_theta[k].astype(F32)
    mean_delta = anchor[...] - total / n_island
    momentum_new = outer_beta * momentum[...] + mean_delta
    momentum_out[...] = momentum_new
    anchor_out[...] = anchor[...] - outer_rate * (mean_delta + outer_beta * momentum_new)

    for step in range(n_island):
        arrived(step, send_sem).wait()
        pass_on(step).wait_send()
        share_theta(step).wait_send()
        share_grad(step).wait_send()
        if step < n_island - 1:
            share_island(step).wait_send()


def per_device(
    n_island,
    n_expert,
    theta,
    first_moment,
    second_moment,
    anchor,
    momentum,
    cotangent,
    weights,
    expert_ids,
    expert_counts,
    hidden_saved,
):
    n = n_island
    theta_rows, features = theta.shape[2:]
    width = features // n
    slots, units = hidden_saved.shape[3:]
    experts = n_expert // HALVES
    tokens = cotangent.shape[0]
    dma = pltpu.SemaphoreType.DMA
    vmem = pl.BlockSpec(memory_space=pltpu.VMEM)
    hbm = pl.BlockSpec(memory_space=pl.ANY)
    anchor_new, momentum_new, d_hidden = pl.pallas_call(
        functools.partial(body, n_island, n_expert),
        out_shape=(
            jax.ShapeDtypeStruct((theta_rows, width), F32),
            jax.ShapeDtypeStruct((theta_rows, width), F32),
            jax.ShapeDtypeStruct((slots, units), BF16),
        ),
        in_specs=[vmem] * 3 + [hbm] * 7,
        out_specs=(vmem,) * 3,
        scratch_shapes=[
            pltpu.VMEM((tokens, features), BF16),
            pltpu.VMEM((slots, units), BF16),
            pltpu.VMEM((units, slots), BF16),
            pltpu.VMEM((theta_rows, features), BF16),
            pltpu.VMEM((theta_rows, features), BF16),
            pltpu.VMEM((theta_rows, width), F32),
            pltpu.VMEM((theta_rows, width), F32),
            pltpu.VMEM((3, experts * CAP, tokens), BF16),
            pltpu.VMEM((n, experts, CAP, width), BF16),
            pltpu.VMEM((n, HALVES, slots // HALVES, width), BF16),
            pltpu.VMEM((n, 2, theta_rows, width), BF16),
            pltpu.VMEM((n, 2, theta_rows, width), BF16),
            pltpu.VMEM((n, theta_rows, width), BF16),
            pltpu.VMEM((n, theta_rows, width), BF16),
            pltpu.VMEM((n, theta_rows, width), BF16),
            pltpu.VMEM((slots, units), F32),
            dma((5,)),
            dma,
            dma((n,)),
            dma((n,)),
            dma((n,)),
            dma((n,)),
            dma((n,)),
            dma((n,)),
            dma((n,)),
            dma((n,)),
            dma((n,)),
            dma((n,)),
            dma((n,)),
        ],
        compiler_params=pltpu.CompilerParams(
            collective_id=0, has_side_effects=True, vmem_limit_bytes=48 << 20
        ),
        name="diloco_step",
    )(
        expert_ids.T,
        weights.T,
        expert_counts,
        theta.reshape(theta_rows, features),
        first_moment.reshape(theta_rows, features),
        second_moment.reshape(theta_rows, features),
        anchor.reshape(theta_rows, width),
        momentum.reshape(theta_rows, width),
        cotangent,
        hidden_saved.reshape(slots, units),
    )
    return (
        anchor_new.reshape(anchor.shape),
        momentum_new.reshape(momentum.shape),
        d_hidden.reshape(hidden_saved.shape),
    )


def solution(mesh):
    return jax.shard_map(
        functools.partial(per_device, mesh.shape["island"], mesh.shape["expert"]),
        mesh=mesh,
        in_specs=(
            P("island", "expert", "dp", None),
            P("island", "expert", "dp", None),
            P("island", "expert", "dp", None),
            P("expert", "dp", "island"),
            P("expert", "dp", "island"),
            P(("island", "dp", "expert"), None),
            P(("island", "dp", "expert"), None),
            P(("island", "dp", "expert"), None),
            P(("island", "dp", "expert"), None),
            P("island", "dp", "expert", None, None),
        ),
        out_specs=(
            P("expert", "dp", "island"),
            P("expert", "dp", "island"),
            P("island", "dp", "expert", None, None),
        ),
        check_vma=False,
    )
```

time: 272 us -> 96.1 us (0.35)
  blocking collectives: 115 us -> 0 us
  waiting for transfers between devices: 97.1 us -> 0 us
  Pallas kernels: 0 us -> 84.9 us
  local copies, waits for them, and re-layouts: 25.8 us -> 10.1 us
  between operations: 15.8 us -> 0.68 us
  other arithmetic: 12.7 us -> 0 us
  matrix products: 4.73 us -> 0 us
    all_to_all x1 -> x0, blocking collectives: 115 us -> none  [per_device(): lax.all_to_all(doubled, 'expert', split_axis=0, concat_axis=0, tiled=True)]
    pallas_call x0 -> x1, Pallas kernels: none -> 84.9 us  [per_device(): pl.pallas_call(functools.partial(body, n_island, n_expert), out_shape=(ja...]
    reduce_scatter x1 -> x0, waiting for transfers between devices: 40.1 us -> none  [per_device(): lax.psum_scatter(island_delta, 'island', scatter_dimension=1, tiled=True)]
    all_gather x2 -> x0, waiting for transfers between devices: 29.9 us -> none  [the longest x1 29.9 us: per_device(): lax.all_gather(local_theta, 'dp', axis=0, tiled=True)]
    unnamed x5 -> x0, waiting for transfers between devices: 27.1 us -> none
    scatter x2 -> x0, local copies, waits for them, and re-layouts: 8.61 us -> none  [the longest x1 4.3 us: pack_rows(): jnp.zeros((window_experts * capacity + 1,), jnp.int32).at[slot_index]]
    sub x1 -> x0, other arithmetic: 5.26 us -> none  [per_device(): island_delta = full_anchor - theta_new.astype(jnp.float32)]
    dot_general x2 -> x0, matrix products: 4.73 us -> none  [the longest x1 3.43 us: per_device(): lax.dot_general(slot_rows, lax.all_gather(local_theta, 'dp', axis=0, tile...]
  transfers between devices with their start and end apart: 4 -> 0, of which waited for: 3 -> 0; matrix products, arithmetic and copies ran while one was open for 6% -> 0% of each run, Pallas kernels for 0% -> 0%
where the time goes in v1:
time: 96.1 us; the launch traced here: 95.7 us
  Pallas kernels  84.9 us (88%)
  local copies, waits for them, and re-layouts  10.1 us (11%)
    pallas_call x1, Pallas kernels, per_device(): pl.pallas_call(functools.partial(body, n_island, n_expert), out_shape=(ja...  84.9 us
    unnamed x23, local copies, waits for them, and re-layouts  10.1 us

profile of v1, /device:TPU:1, one launch (start us, length us, event | category | flops | bytes accessed | tf_op | source)
XLA Modules:
  0.0 95.7 jit_solution(16100884841837306440)
XLA Ops:
  0.6 0.0 copy-start.8
  0.6 0.0 copy-start.7
  0.7 0.0 copy-start.9
  0.7 0.7 copy-done.8
  1.3 0.0 copy-done.7
  1.3 0.0 copy-done.9
  1.3 0.0 copy-start
  1.3 1.1 %copy-done = bf16[1,1,192,2048]{3,2,1,0:T(8,128)(2,1)S(1)} copy-done((bf16[1,1,192,2048]{3,2,1,0:T(8,128)(2,1)S(1)}, bf16[1,1,192,2048]{3,2,1,0:T(8,128)(2,1)}, u32[]{:S(2)}) %copy-start) | copy-done | bytes 786456
  2.5 0.0 copy-start.1
  2.5 1.1 %copy-done.1 = bf16[1,1,192,2048]{3,2,1,0:T(8,128)(2,1)S(1)} copy-done((bf16[1,1,192,2048]{3,2,1,0:T(8,128)(2,1)S(1)}, bf16[1,1,192,2048]{3,2,1,0:T(8,128)(2,1)}, u32[]{:S(2)}) %copy-start.1) | copy-done | bytes 786456
  3.6 0.0 copy-start.2
  3.6 1.1 %copy-done.2 = bf16[1,1,192,2048]{3,2,1,0:T(8,128)(2,1)S(1)} copy-done((bf16[1,1,192,2048]{3,2,1,0:T(8,128)(2,1)S(1)}, bf16[1,1,192,2048]{3,2,1,0:T(8,128)(2,1)}, u32[]{:S(2)}) %copy-start.2) | copy-done | bytes 786456
  4.7 0.0 copy-start.3
  4.7 1.0 %copy-done.3 = bf16[128,2048]{1,0:T(8,128)(2,1)S(1)} copy-done((bf16[128,2048]{1,0:T(8,128)(2,1)S(1)}, bf16[128,2048]{1,0:T(8,128)(2,1)}, u32[]{:S(2)}) %copy-start.3) | copy-done | bytes 524312
  5.8 0.0 copy-start.4
  5.8 1.0 %copy-done.4 = bf16[1,1,1,512,384]{4,3,2,1,0:T(8,128)(2,1)S(1)} copy-done((bf16[1,1,1,512,384]{4,3,2,1,0:T(8,128)(2,1)S(1)}, bf16[1,1,1,512,384]{4,3,2,1,0:T(8,128)(2,1)}, u32[]{:S(2)}) %copy-start.4) | copy-done | bytes 393240
  6.8 0.0 copy-start.5
  6.8 0.9 copy-done.5
  7.7 0.0 copy-start.6
  7.7 0.9 copy-done.6
  8.6 84.9 %diloco_step.1 = (f32[192,256]{1,0:T(8,128)S(1)}, f32[192,256]{1,0:T(8,128)S(1)}, bf16[512,384]{1,0:T(8,128)(2,1)S(1)}) custom-call(s32[8,128]{1,0:T(8,128)S(1)} %bitcast.20, f32[8,128]{1,0:T(8,128)S(1)} %bitcast.21, s32[1,16]{1,0:T(1,128)S(1)} %copy-done.9, bf16[192,2048]{1,0:T(8,128)(2,1)S(1)} %bitcast.11, bf16[192,2048]{1,0:T(8,128)(2,1)S(1)} %bitcast.12, ...), custom_call_target="tpu_custom_call" | custom-call | tf_op jit(solution)/shard_map/diloco_step/pallas_call | solution.py:411
  93.6 0.7 copy.16
  94.2 0.7 copy.17
  94.9 0.7 copy.18
Async XLA Ops:
  0.6 0.7 copy-start.8
  0.6 0.7 copy-start.7
  0.7 0.7 copy-start.9
  1.3 1.1 %copy-start = (bf16[1,1,192,2048]{3,2,1,0:T(8,128)(2,1)S(1)}, bf16[1,1,192,2048]{3,2,1,0:T(8,128)(2,1)}, u32[]{:S(2)}) copy-start(bf16[1,1,192,2048]{3,2,1,0:T(8,128)(2,1)} %param.10) | copy-start | bytes 2359300
  2.5 1.1 %copy-start.1 = (bf16[1,1,192,2048]{3,2,1,0:T(8,128)(2,1)S(1)}, bf16[1,1,192,2048]{3,2,1,0:T(8,128)(2,1)}, u32[]{:S(2)}) copy-start(bf16[1,1,192,2048]{3,2,1,0:T(8,128)(2,1)} %param.11) | copy-start | bytes 2359300
  3.6 1.1 %copy-start.2 = (bf16[1,1,192,2048]{3,2,1,0:T(8,128)(2,1)S(1)}, bf16[1,1,192,2048]{3,2,1,0:T(8,128)(2,1)}, u32[]{:S(2)}) copy-start(bf16[1,1,192,2048]{3,2,1,0:T(8,128)(2,1)} %param.12) | copy-start | bytes 2359300
  4.7 1.0 %copy-start.3 = (bf16[128,2048]{1,0:T(8,128)(2,1)S(1)}, bf16[128,2048]{1,0:T(8,128)(2,1)}, u32[]{:S(2)}) copy-start(bf16[128,2048]{1,0:T(8,128)(2,1)} %cot_hbm.1) | copy-start | bytes 1572868
  5.8 1.0 %copy-start.4 = (bf16[1,1,1,512,384]{4,3,2,1,0:T(8,128)(2,1)S(1)}, bf16[1,1,1,512,384]{4,3,2,1,0:T(8,128)(2,1)}, u32[]{:S(2)}) copy-start(bf16[1,1,1,512,384]{4,3,2,1,0:T(8,128)(2,1)} %param.19) | copy-start | bytes 1179652
  6.8 0.9 copy-start.5
  7.7 0.9 copy-start.6

commit v2 on v1

--- a/solution.py
+++ b/solution.py
@@ -11,7 +11,8 @@
 CAP = 16
 HALVES = 2
 GROUPS = 2
-AHEAD = 2
+LAST = 1
+AHEAD = 3
 
 beta_one = 0.9
 beta_two = 0.95
@@ -21,6 +22,7 @@
 outer_beta = 0.9
 outer_rate = 0.7
 
+VMEM_LIMIT = 48 << 20
 MESH = pl.DeviceIdType.MESH
 F32 = jnp.float32
 BF16 = jnp.bfloat16
@@ -33,9 +35,9 @@
 def body(
     n_island,
     n_expert,
-    ids_ref,
-    weights_ref,
-    counts_ref,
+    ids_hbm,
+    weights_hbm,
+    counts_hbm,
     theta_hbm,
     first_hbm,
     second_hbm,
@@ -46,6 +48,9 @@
     anchor_out,
     momentum_out,
     hidden_out,
+    ids_ref,
+    weights_ref,
+    counts_ref,
     cot,
     saved,
     saved_t,
@@ -55,10 +60,15 @@
     momentum,
     picks,
     packed,
+    packed_last,
     slots,
+    slots_last,
     thetas,
+    thetas_last,
     partial,
+    partial_last,
     partner_partial,
+    partner_partial_last,
     new_theta,
     all_theta,
     hidden_acc,
@@ -82,7 +92,10 @@
     per_half = ring // HALVES
     experts = GROUPS * pairs
     rows = GROUPS * per_half * CAP
-    width = cot.shape[1] // n_island
+    away = n_island - 1
+    steps = away + LAST
+    share = cot.shape[1] // n_island
+    narrow = share // LAST
     theta_rows = thetas.shape[2]
     tokens = cot.shape[0]
     scale = FF ** (-0.5)
@@ -97,14 +110,25 @@
     partner = group * ring + pair * HALVES + (1 - half)
     other_dp = 1 - dp
 
+    def last(step):
+        return isinstance(step, int) and step >= away
+
     def columns(step):
-        chunk = (island + 1 + step) % n_island
-        return pl.ds(pl.multiple_of(chunk * width, width), width)
+        if last(step):
+            start = island * share + (step - away) * narrow
+            return pl.ds(pl.multiple_of(start, narrow), narrow)
+        return pl.ds(pl.multiple_of((island + 1 + step) % n_island * share, share), share)
+
+    def of(wide, cut, step):
+        return cut.at[step - away] if last(step) else wide.at[step]
 
     loads = [
         pltpu.make_async_copy(src, dst, load_sem.at[k])
         for k, (src, dst) in enumerate(
             [
+                (ids_hbm, ids_ref),
+                (weights_hbm, weights_ref),
+                (counts_hbm, counts_ref),
                 (cot_hbm, cot),
                 (first_hbm, first),
                 (second_hbm, second),
@@ -113,7 +137,8 @@
             ]
         )
     ]
-    loads[0].start()
+    for load in loads[:4]:
+        load.start()
 
     barrier = pltpu.get_barrier_semaphore()
     greeted = 0
@@ -141,11 +166,8 @@
 
     def theta_load(step):
         return pltpu.make_async_copy(
-            theta_hbm.at[:, columns(step)], thetas.at[step, dp], theta_sem.at[step]
-        )
-
-    for step in range(n_island):
-        theta_load(step).start()
+            theta_hbm.at[:, columns(step)], of(thetas, thetas_last, step).at[dp], theta_sem.at[step]
+        )
 
     def canonical(k):
         which = k // (GROUPS * per_half)
@@ -164,10 +186,8 @@
         ).start()
         return carry
 
-    lax.fori_loop(0, blocks, load_saved, 0)
-    for load in loads[1:]:
-        load.start()
-
+    for load in loads[:3]:
+        load.wait()
     ids = ids_ref[...]
     weights = weights_ref[...]
     expert_of = lax.broadcasted_iota(jnp.int32, (experts, tokens), 0)
@@ -207,8 +227,10 @@
     def pack(step):
         chunk = cot[:, columns(step)]
         rows_out = sum(dot(picks[k], chunk, ((1,), (0,))) for k in range(3))
-        packed[step] = rows_out.astype(BF16).reshape(experts, CAP, width)
-        slots[step, half, pl.ds(pl.multiple_of(own_row, CAP), CAP), :] = packed[step, own_expert]
+        to = of(packed, packed_last, step)
+        to[...] = rows_out.astype(BF16).reshape(experts, CAP, -1)
+        own = of(slots, slots_last, step).at[half, pl.ds(pl.multiple_of(own_row, CAP), CAP)]
+        own[...] = to[own_expert]
 
     def sends(step):
         copies = []
@@ -228,8 +250,10 @@
                 row = (group * per_half + place) * CAP
                 copies.append(
                     pltpu.make_async_remote_copy(
-                        packed.at[step, to_group * pairs + to_pair],
-                        slots.at[step, to_half, pl.ds(pl.multiple_of(row, CAP), CAP)],
+                        of(packed, packed_last, step).at[to_group * pairs + to_pair],
+                        of(slots, slots_last, step).at[
+                            to_half, pl.ds(pl.multiple_of(row, CAP), CAP)
+                        ],
                         send_sem.at[step],
                         recv_sem.at[step],
                         device_id={"expert": to_group * ring + to_pair * HALVES + to_half},
@@ -243,13 +267,13 @@
             copy.start()
 
     def arrived(step, sem):
-        some = slots.at[step, 0, pl.ds(0, rows - CAP)]
+        some = of(slots, slots_last, step).at[0, pl.ds(0, rows - CAP)]
         return pltpu.make_async_copy(some, some, sem.at[step])
 
     def pass_on(step):
         return pltpu.make_async_remote_copy(
-            slots.at[step, half],
-            slots.at[step, half],
+            of(slots, slots_last, step).at[half],
+            of(slots, slots_last, step).at[half],
             pass_send.at[step],
             pass_recv.at[step],
             device_id={"expert": partner},
@@ -258,8 +282,8 @@
 
     def share_theta(step):
         return pltpu.make_async_remote_copy(
-            thetas.at[step, dp],
-            thetas.at[step, dp],
+            of(thetas, thetas_last, step).at[dp],
+            of(thetas, thetas_last, step).at[dp],
             theta_send.at[step],
             theta_recv.at[step],
             device_id={"dp": other_dp},
@@ -268,8 +292,8 @@
 
     def share_grad(step):
         return pltpu.make_async_remote_copy(
-            partial.at[step, other_dp],
-            partner_partial.at[step],
+            of(partial, partial_last, step).at[other_dp],
+            of(partner_partial, partner_partial_last, step),
             grad_send.at[step],
             grad_recv.at[step],
             device_id={"dp": other_dp},
@@ -288,101 +312,140 @@
         )
 
     def contract(step):
-        chunk = slots[step].reshape(HALVES * rows, width)
+        pass_on(step).wait_recv()
+        chunk = of(slots, slots_last, step)[...].reshape(HALVES * rows, -1)
         product = (scale * dot(saved_t[...], chunk, ((1,), (0,)))).astype(BF16)
-        partial[step, 0] = product[:theta_rows]
-        partial[step, 1] = product[theta_rows:]
+        to = of(partial, partial_last, step)
+        to[0] = product[:theta_rows]
+        to[1] = product[theta_rows:]
         share_grad(step).start()
         share_theta(step).wait_recv()
-        full = thetas[step].reshape(2 * theta_rows, width)
+        full = of(thetas, thetas_last, step)[...].reshape(2 * theta_rows, -1)
         hidden_acc[...] += dot(chunk, full, ((1,), (1,)))
 
     def update(step):
         share_grad(step).wait_recv()
-        grad = partial[step, dp].astype(F32) + partner_partial[step].astype(F32)
+        mine = of(partial, partial_last, step)[dp].astype(F32)
+        grad = mine + of(partner_partial, partner_partial_last, step)[...].astype(F32)
         first_new = beta_one * first[:, columns(step)].astype(F32) + (1.0 - beta_one) * grad
         second_new = (
             beta_two * second[:, columns(step)].astype(F32) + (1.0 - beta_two) * grad * grad
         )
-        wide = thetas[step, dp].astype(F32)
+        wide = of(thetas, thetas_last, step)[dp].astype(F32)
         step_size = first_new / (jnp.sqrt(second_new) + adam_epsilon) + decay_rate * wide
         return (wide - inner_rate * step_size).astype(BF16)
 
-    loads[0].wait()
-    for step in range(AHEAD):
+    def update_away(step):
+        new_theta[step] = update(step)
+        share_island(step).start()
+
+    loads[3].wait()
+    pack(0)
+    pl.semaphore_wait(barrier, greeted)
+    send(0)
+    for step in range(1, min(AHEAD, steps)):
         pack(step)
-
-    pl.semaphore_wait(barrier, greeted)
-    for step in range(AHEAD):
         send(step)
 
-    for step in range(n_island):
+    for step in range(steps):
+        theta_load(step).start()
+    lax.fori_loop(0, blocks, load_saved, 0)
+    for load in loads[4:]:
+        load.start()
+    hidden_acc[...] = jnp.zeros_like(hidden_acc)
+    for step in range(steps):
         theta_load(step).wait()
+    for step in range(min(AHEAD, steps)):
         share_theta(step).start()
-
     pltpu.make_async_copy(saved, saved, saved_sem).wait()
     saved_t[...] = saved[...].T
-    hidden_acc[...] = jnp.zeros_like(hidden_acc)
-    for load in loads[1:]:
+    for load in loads[4:]:
         load.wait()
 
+    def pass_along(step):
+        arrived(step, recv_sem).wait()
+        pass_on(step).start()
+
+    def advance(step):
+        share_theta(step).start()
+        pack(step)
+        send(step)
+
     def run(t, carry):
-        @pl.when(t + AHEAD < n_island)
+        pass_along(t)
+
+        @pl.when(t + AHEAD < away)
         def _():
-            pack(t + AHEAD)
-            send(t + AHEAD)
-
-        @pl.when(t < n_island)
+            advance(t + AHEAD)
+
+        for step in range(away, steps):
+
+            @pl.when(t + AHEAD == step)
+            def _():
+                advance(step)
+
+        @pl.when(t >= 1)
         def _():
-            arrived(t, recv_sem).wait()
-            pass_on(t).start()
-
-        @pl.when((t >= 1) & (t <= n_island))
-        def _():
-            pass_on(t - 1).wait_recv()
             contract(t - 1)
 
         @pl.when(t >= 2)
         def _():
-            fresh = update(t - 2)
-
-            @pl.when(t < n_island + 1)
-            def _():
-                new_theta[t - 2] = fresh
-                share_island(t - 2).start()
-
-            @pl.when(t == n_island + 1)
-            def _():
-                all_theta[island] = fresh
+            update_away(t - 2)
 
         return carry
 
-    lax.fori_loop(0, n_island + 2, run, 0)
+    lax.fori_loop(0, away, run, 0)
+    for step in range(away + AHEAD, steps):
+        advance(step)
+
+    pass_along(away)
+    contract(away - 1)
+    if away >= 2:
+        update_away(away - 2)
+    for step in range(away + 1, steps):
+        pass_along(step)
+    update_away(away - 1)
+    for step in range(away, steps):
+        contract(step)
+
+    others = jnp.zeros((theta_rows, share), F32)
+    for hop in range(1, n_island):
+        source = (island + hop) % n_island
+        landed = all_theta.at[source]
+        pltpu.make_async_copy(landed, landed, island_recv.at[source]).wait()
+        others += landed[...].astype(F32)
 
     for k in range(blocks):
         at = pl.ds(pl.multiple_of(canonical(k) * CAP, CAP), CAP)
         hidden_out[at, :] = (scale * hidden_acc[k * CAP : (k + 1) * CAP, :]).astype(BF16)
 
-    for k in range(1, n_island):
-        source = (island + k) % n_island
-        pltpu.make_async_copy(
-            all_theta.at[source], all_theta.at[source], island_recv.at[source]
-        ).wait()
-    total = all_theta[0].astype(F32)
-    for k in range(1, n_island):
-        total += all_theta[k].astype(F32)
-    mean_delta = anchor[...] - total / n_island
-    momentum_new = outer_beta * momentum[...] + mean_delta
-    momentum_out[...] = momentum_new
-    anchor_out[...] = anchor[...] - outer_rate * (mean_delta + outer_beta * momentum_new)
-
-    for step in range(n_island):
+    for step in range(away, steps):
+        at = slice((step - away) * narrow, (step - away + 1) * narrow)
+        mean_delta = anchor[:, at] - (others[:, at] + update(step).astype(F32)) / n_island
+        momentum_new = outer_beta * momentum[:, at] + mean_delta
+        momentum_out[:, at] = momentum_new
+        anchor_out[:, at] = anchor[:, at] - outer_rate * (mean_delta + outer_beta * momentum_new)
+
+    for step in range(steps):
         arrived(step, send_sem).wait()
         pass_on(step).wait_send()
         share_theta(step).wait_send()
         share_grad(step).wait_send()
-        if step < n_island - 1:
+        if step < away:
             share_island(step).wait_send()
+
+
+def store(anchor, momentum, hidden, anchor_hbm, momentum_hbm, hidden_hbm, sems):
+    copies = [
+        pltpu.make_async_copy(src, dst, sems.at[k])
+        for k, (src, dst) in enumerate(
+            [(anchor, anchor_hbm), (momentum, momentum_hbm), (hidden, hidden_hbm)]
+        )
+    ]
+    for copy in copies:
+        copy.start()
+    for copy in copies:
+        copy.wait()
 
 
 def per_device(
@@ -399,71 +462,97 @@
     expert_counts,
     hidden_saved,
 ):
-    n = n_island
+    away = n_island - 1
+    steps = away + LAST
     theta_rows, features = theta.shape[2:]
-    width = features // n
+    share = features // n_island
+    narrow = share // LAST
     slots, units = hidden_saved.shape[3:]
     experts = n_expert // HALVES
-    tokens = cotangent.shape[0]
+    tokens, top = expert_ids.shape
     dma = pltpu.SemaphoreType.DMA
+
+    def both(*shape):
+        return (
+            pltpu.VMEM((away, *shape, share), BF16),
+            pltpu.VMEM((LAST, *shape, narrow), BF16),
+        )
+
     vmem = pl.BlockSpec(memory_space=pltpu.VMEM)
-    hbm = pl.BlockSpec(memory_space=pl.ANY)
-    anchor_new, momentum_new, d_hidden = pl.pallas_call(
+    hbm = pl.BlockSpec(memory_space=pltpu.HBM)
+    results = (
+        jax.ShapeDtypeStruct((theta_rows, share), F32),
+        jax.ShapeDtypeStruct((theta_rows, share), F32),
+        jax.ShapeDtypeStruct((slots, units), BF16),
+    )
+    fresh = pl.pallas_call(
         functools.partial(body, n_island, n_expert),
-        out_shape=(
-            jax.ShapeDtypeStruct((theta_rows, width), F32),
-            jax.ShapeDtypeStruct((theta_rows, width), F32),
-            jax.ShapeDtypeStruct((slots, units), BF16),
-        ),
-        in_specs=[vmem] * 3 + [hbm] * 7,
+        out_shape=results,
+        in_specs=[hbm] * 10,
         out_specs=(vmem,) * 3,
         scratch_shapes=[
+            pltpu.VMEM((top, tokens), jnp.int32),
+            pltpu.VMEM((top, tokens), F32),
+            pltpu.VMEM((1, experts), jnp.int32),
             pltpu.VMEM((tokens, features), BF16),
             pltpu.VMEM((slots, units), BF16),
             pltpu.VMEM((units, slots), BF16),
             pltpu.VMEM((theta_rows, features), BF16),
             pltpu.VMEM((theta_rows, features), BF16),
-            pltpu.VMEM((theta_rows, width), F32),
-            pltpu.VMEM((theta_rows, width), F32),
+            pltpu.VMEM((theta_rows, share), F32),
+            pltpu.VMEM((theta_rows, share), F32),
             pltpu.VMEM((3, experts * CAP, tokens), BF16),
-            pltpu.VMEM((n, experts, CAP, width), BF16),
-            pltpu.VMEM((n, HALVES, slots // HALVES, width), BF16),
-            pltpu.VMEM((n, 2, theta_rows, width), BF16),
-            pltpu.VMEM((n, 2, theta_rows, width), BF16),
-            pltpu.VMEM((n, theta_rows, width), BF16),
-            pltpu.VMEM((n, theta_rows, width), BF16),
-            pltpu.VMEM((n, theta_rows, width), BF16),
+            *both(experts, CAP),
+            *both(HALVES, slots // HALVES),
+            *both(2, theta_rows),
+            *both(2, theta_rows),
+            *both(theta_rows),
+            pltpu.VMEM((away, theta_rows, share), BF16),
+            pltpu.VMEM((n_island, theta_rows, share), BF16),
             pltpu.VMEM((slots, units), F32),
-            dma((5,)),
+            dma((8,)),
             dma,
-            dma((n,)),
-            dma((n,)),
-            dma((n,)),
-            dma((n,)),
-            dma((n,)),
-            dma((n,)),
-            dma((n,)),
-            dma((n,)),
-            dma((n,)),
-            dma((n,)),
-            dma((n,)),
+            dma((steps,)),
+            dma((steps,)),
+            dma((steps,)),
+            dma((steps,)),
+            dma((steps,)),
+            dma((steps,)),
+            dma((steps,)),
+            dma((steps,)),
+            dma((steps,)),
+            dma((steps,)),
+            dma((n_island,)),
         ],
         compiler_params=pltpu.CompilerParams(
-            collective_id=0, has_side_effects=True, vmem_limit_bytes=48 << 20
+            collective_id=0, has_side_effects=True, vmem_limit_bytes=VMEM_LIMIT
         ),
         name="diloco_step",
     )(
-        expert_ids.T,
-        weights.T,
-        expert_counts,
-        theta.reshape(theta_rows, features),
-        first_moment.reshape(theta_rows, features),
-        second_moment.reshape(theta_rows, features),
-        anchor.reshape(theta_rows, width),
-        momentum.reshape(theta_rows, width),
-        cotangent,
-        hidden_saved.reshape(slots, units),
+        *(
+            pltpu.with_memory_space_constraint(x, pltpu.HBM)
+            for x in (
+                expert_ids.T,
+                weights.T,
+                expert_counts,
+                theta.reshape(theta_rows, features),
+                first_moment.reshape(theta_rows, features),
+                second_moment.reshape(theta_rows, features),
+                anchor.reshape(theta_rows, share),
+                momentum.reshape(theta_rows, share),
+                cotangent,
+                hidden_saved.reshape(slots, units),
+            )
+        )
     )
+    anchor_new, momentum_new, d_hidden = pl.pallas_call(
+        store,
+        out_shape=results,
+        in_specs=[vmem] * 3,
+        out_specs=(hbm,) * 3,
+        scratch_shapes=[dma((3,))],
+        name="store",
+    )(*(pltpu.with_memory_space_constraint(x, pltpu.VMEM) for x in fresh))
     return (
         anchor_new.reshape(anchor.shape),
         momentum_new.reshape(momentum.shape),

time: 96.1 us -> 86.1 us (0.90)
  local copies, waits for them, and re-layouts: 10.1 us -> 0 us
    unnamed x23 -> x0, local copies, waits for them, and re-layouts: 10.1 us -> none
    pallas_call x1 -> x2, Pallas kernels: 84.9 us -> 85.3 us  [the longest x1 84.4 us: per_device(): pl.pallas_call(functools.partial(body, n_island, n_expert), out_shape=res...]
where the time goes in v2:
time: 86.1 us; the launch traced here: 85.9 us
  Pallas kernels  85.3 us (99%)
    pallas_call x1, Pallas kernels, per_device(): pl.pallas_call(functools.partial(body, n_island, n_expert), out_shape=res...  84.4 us

profile of v2, /device:TPU:1, one launch (start us, length us, event | category | flops | bytes accessed | tf_op | source)
XLA Modules:
  0.0 85.9 jit_solution(10088047743342418444)
XLA Ops:
  0.6 84.4 %diloco_step.1 = (f32[192,256]{1,0:T(8,128)S(1)}, f32[192,256]{1,0:T(8,128)S(1)}, bf16[512,384]{1,0:T(8,128)(2,1)S(1)}) custom-call(s32[8,128]{1,0:T(8,128)} %bitcast.17, f32[8,128]{1,0:T(8,128)} %bitcast.18, s32[1,16]{1,0:T(1,128)} %counts_hbm.1, bf16[192,2048]{1,0:T(8,128)(2,1)} %bitcast.11, bf16[192,2048]{1,0:T(8,128)(2,1)} %bitcast.12, ...), custom_call_target="tpu_custom_call" | custom-call | tf_op jit(solution)/shard_map/diloco_step/pallas_call | solution.py:488
  85.0 0.9 %store.1 = (f32[192,256]{1,0:T(8,128)}, f32[192,256]{1,0:T(8,128)}, bf16[512,384]{1,0:T(8,128)(2,1)}) custom-call(f32[192,256]{1,0:T(8,128)S(1)} %get-tuple-element.9.anchor, f32[192,256]{1,0:T(8,128)S(1)} %get-tuple-element.10.momentum, bf16[512,384]{1,0:T(8,128)(2,1)S(1)} %get-tuple-element.11.hidden), custom_call_target="tpu_custom_call" | custom-call | tf_op jit(solution)/shard_map/store/pallas_call | solution.py:548

commit v3 on v2

--- a/solution.py
+++ b/solution.py
@@ -9,10 +9,12 @@
 
 FF = 768
 CAP = 16
+CORES = 2
 HALVES = 2
 GROUPS = 2
 LAST = 1
 AHEAD = 3
+AHEAD_LAST = 3
 
 beta_one = 0.9
 beta_two = 0.95
@@ -110,6 +112,11 @@
     partner = group * ring + pair * HALVES + (1 - half)
     other_dp = 1 - dp
 
+    def owner_of(step):
+        apart = n_island - 1 - step
+        chip = (island // CORES + apart // CORES) % (n_island // CORES)
+        return chip * CORES + (island % CORES + apart % CORES) % CORES
+
     def last(step):
         return isinstance(step, int) and step >= away
 
@@ -117,7 +124,7 @@
         if last(step):
             start = island * share + (step - away) * narrow
             return pl.ds(pl.multiple_of(start, narrow), narrow)
-        return pl.ds(pl.multiple_of((island + 1 + step) % n_island * share, share), share)
+        return pl.ds(pl.multiple_of(owner_of(step) * share, share), share)
 
     def of(wide, cut, step):
         return cut.at[step - away] if last(step) else wide.at[step]
@@ -137,8 +144,6 @@
             ]
         )
     ]
-    for load in loads[:4]:
-        load.start()
 
     barrier = pltpu.get_barrier_semaphore()
     greeted = 0
@@ -163,6 +168,9 @@
             barrier, inc=1, device_id={"island": (island + k) % n_island}, device_id_type=MESH
         )
         greeted += 1
+
+    for load in loads[:4]:
+        load.start()
 
     def theta_load(step):
         return pltpu.make_async_copy(
@@ -301,7 +309,7 @@
         )
 
     def share_island(step):
-        owner = (island + 1 + step) % n_island
+        owner = owner_of(step)
         return pltpu.make_async_remote_copy(
             new_theta.at[step],
             all_theta.at[island],
@@ -314,11 +322,15 @@
     def contract(step):
         pass_on(step).wait_recv()
         chunk = of(slots, slots_last, step)[...].reshape(HALVES * rows, -1)
-        product = (scale * dot(saved_t[...], chunk, ((1,), (0,)))).astype(BF16)
         to = of(partial, partial_last, step)
-        to[0] = product[:theta_rows]
-        to[1] = product[theta_rows:]
+
+        def product(part):
+            at = pl.ds(pl.multiple_of(part * theta_rows, theta_rows), theta_rows)
+            return (scale * dot(saved_t[at, :], chunk, ((1,), (0,)))).astype(BF16)
+
+        to[other_dp] = product(other_dp)
         share_grad(step).start()
+        to[dp] = product(dp)
         share_theta(step).wait_recv()
         full = of(thetas, thetas_last, step)[...].reshape(2 * theta_rows, -1)
         hidden_acc[...] += dot(chunk, full, ((1,), (1,)))
@@ -380,7 +392,7 @@
 
         for step in range(away, steps):
 
-            @pl.when(t + AHEAD == step)
+            @pl.when(t + AHEAD_LAST == step)
             def _():
                 advance(step)
 
@@ -395,7 +407,7 @@
         return carry
 
     lax.fori_loop(0, away, run, 0)
-    for step in range(away + AHEAD, steps):
+    for step in range(away + AHEAD_LAST, steps):
         advance(step)
 
     pass_along(away)
@@ -404,9 +416,14 @@
         update_away(away - 2)
     for step in range(away + 1, steps):
         pass_along(step)
+    contract(away)
     update_away(away - 1)
-    for step in range(away, steps):
+    for step in range(away + 1, steps):
         contract(step)
+
+    for k in range(blocks):
+        at = pl.ds(pl.multiple_of(canonical(k) * CAP, CAP), CAP)
+        hidden_out[at, :] = (scale * hidden_acc[k * CAP : (k + 1) * CAP, :]).astype(BF16)
 
     others = jnp.zeros((theta_rows, share), F32)
     for hop in range(1, n_island):
@@ -414,17 +431,6 @@
         landed = all_theta.at[source]
         pltpu.make_async_copy(landed, landed, island_recv.at[source]).wait()
         others += landed[...].astype(F32)
-
-    for k in range(blocks):
-        at = pl.ds(pl.multiple_of(canonical(k) * CAP, CAP), CAP)
-        hidden_out[at, :] = (scale * hidden_acc[k * CAP : (k + 1) * CAP, :]).astype(BF16)
-
-    for step in range(away, steps):
-        at = slice((step - away) * narrow, (step - away + 1) * narrow)
-        mean_delta = anchor[:, at] - (others[:, at] + update(step).astype(F32)) / n_island
-        momentum_new = outer_beta * momentum[:, at] + mean_delta
-        momentum_out[:, at] = momentum_new
-        anchor_out[:, at] = anchor[:, at] - outer_rate * (mean_delta + outer_beta * momentum_new)
 
     for step in range(steps):
         arrived(step, send_sem).wait()
@@ -433,6 +439,13 @@
         share_grad(step).wait_send()
         if step < away:
             share_island(step).wait_send()
+
+    for step in range(away, steps):
+        at = slice((step - away) * narrow, (step - away + 1) * narrow)
+        mean_delta = anchor[:, at] - (others[:, at] + update(step).astype(F32)) / n_island
+        momentum_new = outer_beta * momentum[:, at] + mean_delta
+        momentum_out[:, at] = momentum_new
+        anchor_out[:, at] = anchor[:, at] - outer_rate * (mean_delta + outer_beta * momentum_new)
 
 
 def store(anchor, momentum, hidden, anchor_hbm, momentum_hbm, hidden_hbm, sems):

time: 86.1 us -> 84.3 us (0.979); the launches traced: 85.9 us -> 83.1 us
  Pallas kernels: 85.3 us -> 82.4 us
    pallas_call x1, Pallas kernels: 84.4 us -> 81.5 us  [per_device(): pl.pallas_call(functools.partial(body, n_island, n_expert), out_shape=res...]
where the time goes in v3:
time: 84.3 us; the launch traced here: 83.1 us
  Pallas kernels  82.4 us (98%)
    pallas_call x1, Pallas kernels, per_device(): pl.pallas_call(functools.partial(body, n_island, n_expert), out_shape=res...  81.5 us

profile of v3, /device:TPU:1, one launch (start us, length us, event | category | flops | bytes accessed | tf_op | source)
XLA Modules:
  0.0 83.1 jit_solution(194603101778873993)
XLA Ops:
  0.6 81.5 %diloco_step.1 = (f32[192,256]{1,0:T(8,128)S(1)}, f32[192,256]{1,0:T(8,128)S(1)}, bf16[512,384]{1,0:T(8,128)(2,1)S(1)}) custom-call(s32[8,128]{1,0:T(8,128)} %bitcast.17, f32[8,128]{1,0:T(8,128)} %bitcast.18, s32[1,16]{1,0:T(1,128)} %counts_hbm.1, bf16[192,2048]{1,0:T(8,128)(2,1)} %bitcast.11, bf16[192,2048]{1,0:T(8,128)(2,1)} %bitcast.12, ...), custom_call_target="tpu_custom_call" | custom-call | tf_op jit(solution)/shard_map/diloco_step/pallas_call | solution.py:501
  82.1 0.9 %store.1 = (f32[192,256]{1,0:T(8,128)}, f32[192,256]{1,0:T(8,128)}, bf16[512,384]{1,0:T(8,128)(2,1)}) custom-call(f32[192,256]{1,0:T(8,128)S(1)} %get-tuple-element.9.anchor, f32[192,256]{1,0:T(8,128)S(1)} %get-tuple-element.10.momentum, bf16[512,384]{1,0:T(8,128)(2,1)S(1)} %get-tuple-element.11.hidden), custom_call_target="tpu_custom_call" | custom-call | tf_op jit(solution)/shard_map/store/pallas_call | solution.py:561

commit v4 on v3

--- a/solution.py
+++ b/solution.py
@@ -263,7 +263,7 @@
                             to_half, pl.ds(pl.multiple_of(row, CAP), CAP)
                         ],
                         send_sem.at[step],
-                        recv_sem.at[step],
+                        recv_sem.at[step, other],
                         device_id={"expert": to_group * ring + to_pair * HALVES + to_half},
                         device_id_type=MESH,
                     )
@@ -278,12 +278,19 @@
         some = of(slots, slots_last, step).at[0, pl.ds(0, rows - CAP)]
         return pltpu.make_async_copy(some, some, sem.at[step])
 
-    def pass_on(step):
+    def arrived_from(step, other):
+        size = rows // GROUPS - (CAP if other == 0 else 0)
+        some = of(slots, slots_last, step).at[0, pl.ds(0, size)]
+        return pltpu.make_async_copy(some, some, recv_sem.at[step, other])
+
+    def pass_on(step, other):
+        size = rows // GROUPS
+        at = pl.ds(pl.multiple_of((group + other) % GROUPS * size, size), size)
         return pltpu.make_async_remote_copy(
-            of(slots, slots_last, step).at[half],
-            of(slots, slots_last, step).at[half],
-            pass_send.at[step],
-            pass_recv.at[step],
+            of(slots, slots_last, step).at[half, at],
+            of(slots, slots_last, step).at[half, at],
+            pass_send.at[step, other],
+            pass_recv.at[step, other],
             device_id={"expert": partner},
             device_id_type=MESH,
         )
@@ -320,7 +327,8 @@
         )
 
     def contract(step):
-        pass_on(step).wait_recv()
+        for other in range(GROUPS):
+            pass_on(step, other).wait_recv()
         chunk = of(slots, slots_last, step)[...].reshape(HALVES * rows, -1)
         to = of(partial, partial_last, step)
 
@@ -375,8 +383,9 @@
         load.wait()
 
     def pass_along(step):
-        arrived(step, recv_sem).wait()
-        pass_on(step).start()
+        for other in range(GROUPS):
+            arrived_from(step, other).wait()
+            pass_on(step, other).start()
 
     def advance(step):
         share_theta(step).start()
@@ -434,7 +443,8 @@
 
     for step in range(steps):
         arrived(step, send_sem).wait()
-        pass_on(step).wait_send()
+        for other in range(GROUPS):
+            pass_on(step, other).wait_send()
         share_theta(step).wait_send()
         share_grad(step).wait_send()
         if step < away:
@@ -527,9 +537,9 @@
             dma,
             dma((steps,)),
             dma((steps,)),
-            dma((steps,)),
-            dma((steps,)),
-            dma((steps,)),
+            dma((steps, GROUPS)),
+            dma((steps, GROUPS)),
+            dma((steps, GROUPS)),
             dma((steps,)),
             dma((steps,)),
             dma((steps,)),

time: 84.3 us -> 83.9 us (level)
  no operation moved by 1% of the time
where the time goes in v4:
time: 83.9 us; the launch traced here: 82.8 us
  Pallas kernels  82.1 us (98%)
    pallas_call x1, Pallas kernels, per_device(): pl.pallas_call(functools.partial(body, n_island, n_expert), out_shape=res...  81.2 us

profile of v4, /device:TPU:1, one launch (start us, length us, event | category | flops | bytes accessed | tf_op | source)
XLA Modules:
  0.0 82.8 jit_solution(1611433639209310773)
XLA Ops:
  0.6 81.2 %diloco_step.1 = (f32[192,256]{1,0:T(8,128)S(1)}, f32[192,256]{1,0:T(8,128)S(1)}, bf16[512,384]{1,0:T(8,128)(2,1)S(1)}) custom-call(s32[8,128]{1,0:T(8,128)} %bitcast.17, f32[8,128]{1,0:T(8,128)} %bitcast.18, s32[1,16]{1,0:T(1,128)} %counts_hbm.1, bf16[192,2048]{1,0:T(8,128)(2,1)} %bitcast.11, bf16[192,2048]{1,0:T(8,128)(2,1)} %bitcast.12, ...), custom_call_target="tpu_custom_call" | custom-call | tf_op jit(solution)/shard_map/diloco_step/pallas_call | solution.py:511
  81.9 0.9 %store.1 = (f32[192,256]{1,0:T(8,128)}, f32[192,256]{1,0:T(8,128)}, bf16[512,384]{1,0:T(8,128)(2,1)}) custom-call(f32[192,256]{1,0:T(8,128)S(1)} %get-tuple-element.9.anchor, f32[192,256]{1,0:T(8,128)S(1)} %get-tuple-element.10.momentum, bf16[512,384]{1,0:T(8,128)(2,1)S(1)} %get-tuple-element.11.hidden), custom_call_target="tpu_custom_call" | custom-call | tf_op jit(solution)/shard_map/store/pallas_call | solution.py:571
